TPU v7x, 512 devices: a whole 4x8x8 slice. The times are simulated.
512 devices in a mesh: ctx: 64 (over x, z, core), kvh: 8 (over y).
Axes of the slice: x: 4, y: 8, z: 8, core: 2. Of those that a mesh axis runs over, the one named last changes fastest.
Arguments:
- queries: bfloat16 [32768, 8192], P('ctx', 'kvh')
- key_vector_rows: bfloat16 [32768, 1024], P('ctx', 'kvh')
- value_vector_rows: bfloat16 [32768, 1024], P('ctx', 'kvh'), may hold values from -6 to 6
- block_picks: int32 [256, 8], P('ctx'), may hold values from 0 to 255, as said below
Outputs:
- attended: bfloat16 [32768, 8192], P(('ctx', 'kvh'))
Inputs may be any that keep to these rules, and one draw needn't show every extreme that they name: block_picks[b, 0] = b. The other entries of a row name 7 distinct blocks that lie on other indices of ctx (block c lies on index c // 4). Over the 4 rows of one index of ctx, the entries naming blocks of any one other index are at most 2 and name at most 1 distinct blocks; both bounds are reached in every draw.
All inputs are finite; a program needn't handle non-finite values.
Results may differ from a plain program's by a relative error of at most 0.0047.
Values may be sent and summed in bfloat16 or wider, within the bound.
No kernel may reach another device: no remote copies, remote signals or barrier semaphores. Data moves between devices by JAX's collectives and lax.ppermute only.
A program may use at most 64 MiB of HBM per device.

v0:
```python
import math

import jax
import jax.numpy as jnp
from jax import lax
from jax.sharding import PartitionSpec as P

HEAD_SIZE = 128
BLOCK_TOKENS = 128
PICKED_BLOCKS = 8


def plan_each(remote, blocks, peer_count, capacity):
    flat_picks = remote.reshape(-1)
    owners = flat_picks // blocks
    local_ids = flat_picks % blocks
    owner_hits = (owners[:, None] == jnp.arange(peer_count, dtype=jnp.int32)[None, :]).astype(
        jnp.int32
    )
    running = jnp.cumsum(owner_hits, axis=0) * owner_hits
    slot_rank = jnp.sum(running, axis=1) - 1
    slot_hits = (slot_rank[:, None] == jnp.arange(capacity, dtype=jnp.int32)[None, :]).astype(
        jnp.int32
    )
    requests = jnp.dot((owner_hits * local_ids[:, None]).T, slot_hits)
    return (requests, slot_rank)


def block_attention(query_block, kv_block, kv_heads):
    block_len = query_block.shape[0]
    pick_count = kv_block.shape[0]
    group_size = query_block.shape[1] // (kv_heads * HEAD_SIZE)
    query_heads = query_block.reshape(block_len, kv_heads, group_size, HEAD_SIZE)
    stacked = kv_block.reshape(pick_count * block_len, 2, kv_heads, HEAD_SIZE)
    key_selection = stacked[:, 0]
    value_selection = stacked[:, 1]
    scores = jnp.einsum(
        "qgxd,kgd->gxqk", query_heads, key_selection, preferred_element_type=jnp.float32
    )
    scores = scores * (1.0 / math.sqrt(HEAD_SIZE))
    positions = jnp.arange(block_len, dtype=jnp.int32)
    causal = positions[None, :] <= positions[:, None]
    visible = jnp.concatenate(
        [causal, jnp.ones((block_len, (pick_count - 1) * block_len), dtype=bool)], axis=1
    )
    scores = jnp.where(visible, scores, -jnp.inf)
    row_max = jnp.max(scores, axis=-1, keepdims=True)
    exponents = jnp.exp(scores - row_max)
    totals = jnp.sum(exponents, axis=-1, keepdims=True)
    weights = exponents.astype(jnp.bfloat16)
    blended = jnp.einsum(
        "gxqk,kgd->qgxd", weights, value_selection, preferred_element_type=jnp.float32
    )
    blended = blended / jnp.transpose(totals, (2, 0, 1, 3))
    return blended.reshape(block_len, -1).astype(jnp.bfloat16)


def body(queries, key_vector_rows, value_vector_rows, block_picks):
    peer_count = lax.axis_size("ctx")
    my_index = lax.axis_index("ctx")
    tok_dev = key_vector_rows.shape[0]
    blocks = tok_dev // BLOCK_TOKENS
    kv_heads = key_vector_rows.shape[1] // HEAD_SIZE
    local_kv = jnp.concatenate([key_vector_rows, value_vector_rows], axis=1).reshape(
        blocks, BLOCK_TOKENS, 2 * kv_heads * HEAD_SIZE
    )
    remote = block_picks[:, 1:]
    far_count = blocks * (PICKED_BLOCKS - 1)
    distinct_cap = (far_count // 2 + peer_count - 2) // (peer_count - 1)
    capacity = 2 * distinct_cap
    requests, slot_rank = plan_each(remote, blocks, peer_count, capacity)
    pick_table = lax.all_gather(block_picks, "ctx", axis=0, tiled=True)
    all_rows = pick_table[:, 1:].reshape(peer_count, blocks, PICKED_BLOCKS - 1)

    def requests_of(rows_one):
        return plan_each(rows_one, blocks, peer_count, capacity)[0]

    all_requests = jax.vmap(requests_of)(all_rows)
    wanted = jnp.take(all_requests, my_index, axis=1)
    outgoing = local_kv[wanted]
    incoming = lax.all_to_all(outgoing, "ctx", split_axis=0, concat_axis=0, tiled=True)
    owners = (remote // blocks).reshape(-1)
    fetched = incoming.reshape(peer_count * capacity, BLOCK_TOKENS, -1)[
        owners * capacity + slot_rank
    ]
    fetched = fetched.reshape(blocks, PICKED_BLOCKS - 1, BLOCK_TOKENS, -1)
    chosen = jnp.concatenate([local_kv[:, None], fetched], axis=1)

    def attend_pair(pair):
        return block_attention(pair[0], pair[1], kv_heads)

    attended = lax.map(attend_pair, (queries.reshape(blocks, BLOCK_TOKENS, -1), chosen))
    attended = attended.reshape(tok_dev, -1)
    return lax.all_to_all(attended, "kvh", split_axis=0, concat_axis=1, tiled=True)


def solution(mesh):
    return jax.shard_map(
        body,
        mesh=mesh,
        in_specs=(P("ctx", "kvh"), P("ctx", "kvh"), P("ctx", "kvh"), P("ctx", None)),
        out_specs=P(("ctx", "kvh"), None),
        check_vma=False,
    )
```

profile of v0, /device:TPU:1, one launch (start us, length us, event | category | flops | bytes accessed | tf_op | source)
XLA Modules:
  0.0 326.1 jit_solution(9920349787377583914)
XLA Ops:
  0.0 57.4 %all-gather = s32[64,4,8]{2,1,0:T(4,128)S(1)} all-gather(s32[1,4,8]{2,1,0:T(4,128)} %bitcast.120), channel_id=1, replica_groups=mesh['ctx'=64,'kvh'=8] {'ctx'}, dimensions={0}, use_global_device_ids=true | all-gather | bytes 8320 | tf_op jit(solution)/shard_map/all_gather | solution.py:72
  57.7 1.3 select_reduce_fusion
  59.1 2.6 fusion.19
  62.2 6.3 %gather_fusion = bf16[128,128,256]{2,1,0:T(8,128)(2,1)} fusion(bf16[4,128,256]{2,1,0:T(8,128)(2,1)S(1)} %bitcast.108, s32[1024]{0:T(1024)S(1)} %pad_clamp_fusion.1), kind=kCustom, calls=%fused_computation | custom fusion | bytes 16777728 | tf_op jit(solution)/shard_map/gather | solution.py:80
  68.5 5.9 %all-to-all-start = ((bf16[64,2,128,256]{3,2,1,0:T(8,128)(2,1)}), bf16[64,2,128,256]{3,2,1,0:T(8,128)(2,1)}, u32[]{:S(2)}, u32[]{:S(2)}) async-start(bf16[64,2,128,256]{3,2,1,0:T(8,128)(2,1)} %bitcast.110), calls=%async_computation | async-start | bytes 16777216 | tf_op jit(solution)/shard_map/all_to_all | solution.py:81
  75.0 185.1 %all-to-all-done = bf16[64,2,128,256]{3,2,1,0:T(8,128)(2,1)} async-done(((bf16[64,2,128,256]{3,2,1,0:T(8,128)(2,1)}), bf16[64,2,128,256]{3,2,1,0:T(8,128)(2,1)}, u32[]{:S(2)}, u32[]{:S(2)}) %all-to-all-start) | async-done | bytes 8388640 | tf_op jit(solution)/shard_map/all_to_all | solution.py:81
  260.1 5.4 %gather_fusion.1 = bf16[28,128,256]{2,1,0:T(8,128)(2,1)} fusion(bf16[128,128,256]{2,1,0:T(8,128)(2,1)} %bitcast.22, s32[1024]{0:T(1024)S(1)} %pad_clamp_fusion), kind=kCustom, calls=%fused_computation.1 | custom fusion | bytes 3670128 | tf_op jit(solution)/shard_map/gather | solution.py:83
  265.5 1.7 pad_maximum_fusion
  267.2 21.8 %while.11 = (s32[]{:T(128)}, bf16[4,128,1024]{2,1,0:T(8,128)(2,1)}, bf16[4,8,128,256]{3,2,1,0:T(8,128)(2,1)S(1)}, bf16[4,128,1024]{2,1,0:T(8,128)(2,1)}, s32[]{:T(128)}, /*index=5*/pred[]{:T(512)}) while((s32[]{:T(128)}, bf16[4,128,1024]{2,1,0:T(8,128)(2,1)}, bf16[4,8,128,256]{3,2,1,0:T(8,128)(2,1)S(1)}, bf16[4,128,1024]{2,1,0:T(8,128)(2,1)}, ...), condition=%wide.region_7.8_spmd, body=%wide.region_4.7_spmd.sunk | while | flops 548681728 | bytes 19452492 | solution.py:92
  267.4 0.4 copy.68
  267.8 1.0 constant_dynamic-slice_fusion.4
  269.0 0.7 fusion.44
  269.8 0.9 fusion.45
  270.6 1.1 fusion.46
  271.9 0.7 constant_dynamic-update-slice_fusion.4
  273.3 1.0 constant_dynamic-slice_fusion.4
  274.5 0.7 fusion.44
  275.2 0.9 fusion.45
  276.1 1.1 fusion.46
  277.4 0.7 constant_dynamic-update-slice_fusion.4
  278.7 1.0 constant_dynamic-slice_fusion.4
  279.9 0.7 fusion.44
  280.7 0.9 fusion.45
  281.5 1.1 fusion.46
  282.8 0.7 constant_dynamic-update-slice_fusion.4
  284.1 1.0 constant_dynamic-slice_fusion.4
  285.4 0.7 fusion.44
  286.1 0.9 fusion.45
  287.0 1.1 fusion.46
  288.3 0.7 constant_dynamic-update-slice_fusion.4
  289.0 36.1 %all_to_all.24 = bf16[8,64,1024]{2,1,0:T(8,128)(2,1)S(1)} all-to-all(bf16[8,64,1024]{2,1,0:T(8,128)(2,1)} %bitcast.117), channel_id=1, replica_groups=mesh['ctx'=64,'kvh'=8] {'kvh'}, dimensions={0} | all-to-all | bytes 2097152 | tf_op jit(solution)/shard_map/all_to_all | solution.py:94
  325.1 1.1 copy.61
  (57 shorter events, 4.8 us)
Async XLA Ops:
  0.0 62.1 %copy-start = (bf16[512,128]{1,0:T(8,128)(2,1)S(1)}, bf16[512,128]{1,0:T(8,128)(2,1)}, u32[]{:S(2)}) copy-start(bf16[512,128]{1,0:T(8,128)(2,1)} %param.7) | copy-start | bytes 393220
  0.0 62.1 %copy-start.1 = (bf16[512,128]{1,0:T(8,128)(2,1)S(1)}, bf16[512,128]{1,0:T(8,128)(2,1)}, u32[]{:S(2)}) copy-start(bf16[512,128]{1,0:T(8,128)(2,1)} %param.8) | copy-start | bytes 393220
  68.5 5.9 %copy-start.2 = (s32[4,8]{1,0:T(4,128)S(1)}, s32[4,8]{1,0:T(4,128)}, u32[]{:S(2)}) copy-start(s32[4,8]{1,0:T(4,128)} %param.9) | copy-start | bytes 388
  68.5 191.6 %all-to-all-start = ((bf16[64,2,128,256]{3,2,1,0:T(8,128)(2,1)}), bf16[64,2,128,256]{3,2,1,0:T(8,128)(2,1)}, u32[]{:S(2)}, u32[]{:S(2)}) async-start(bf16[64,2,128,256]{3,2,1,0:T(8,128)(2,1)} %bitcast.110), calls=%async_computation | async-start | bytes 16777216 | tf_op jit(solution)/shard_map/all_to_all | solution.py:81
where the time goes:
time: 327 us; the launch traced here: 326 us
  waiting for transfers between devices  185 us (57%)
  blocking collectives  93.5 us (29%)
  local copies, waits for them, and re-layouts  24.2 us (7%)
  matrix products  10.1 us (3%)
  other arithmetic  6.97 us (2%)
  starting transfers between devices  5.9 us (2%)
    all_to_all x1, waiting for transfers between devices, body(): lax.all_to_all(outgoing, 'ctx', split_axis=0, concat_axis=0, tiled=True)  185 us
    all_gather x1, blocking collectives, body(): pick_table = lax.all_gather(block_picks, 'ctx', axis=0, tiled=True)  57.4 us
    all_to_all x1, blocking collectives, body(): lax.all_to_all(attended, 'kvh', split_axis=0, concat_axis=1, tiled=True)  36.1 us
  transfers between devices with their start and end apart: 1, of which 1 were waited for; matrix products, arithmetic and copies ran while one was open for 0% of the time, Pallas kernels for 0%

commit v1 on v0

v1 whole, which is shorter than its diff:
```python
import math

import jax
import jax.numpy as jnp
from jax import lax
from jax.experimental import pallas as pl
from jax.experimental.pallas import tpu as pltpu
from jax.sharding import PartitionSpec as P

HEAD_SIZE = 128
BLOCK_TOKENS = 128
PICKED_BLOCKS = 8


def pick_kernel(wanted, k_ref, v_ref, out_ref, sem):
    peers = out_ref.shape[0]

    def copies(d):
        start = pl.multiple_of(wanted[d] * BLOCK_TOKENS, BLOCK_TOKENS)
        rows = pl.ds(start, BLOCK_TOKENS)
        return (
            pltpu.make_async_copy(
                k_ref.at[rows], out_ref.at[d, pl.ds(0, BLOCK_TOKENS)], sem
            ),
            pltpu.make_async_copy(
                v_ref.at[rows], out_ref.at[d, pl.ds(BLOCK_TOKENS, BLOCK_TOKENS)], sem
            ),
        )

    @pl.loop(0, peers)
    def _(d):
        for copy in copies(d):
            copy.start()

    pltpu.make_async_copy(out_ref, out_ref, sem).wait()


def pick_blocks(wanted, keys, values):
    peers = wanted.shape[0]
    return pl.pallas_call(
        pick_kernel,
        out_shape=jax.ShapeDtypeStruct((peers, 2 * BLOCK_TOKENS, HEAD_SIZE), keys.dtype),
        grid_spec=pltpu.PrefetchScalarGridSpec(
            num_scalar_prefetch=1,
            grid=(1,),
            in_specs=[
                pl.BlockSpec(keys.shape, lambda i, w: (0, 0)),
                pl.BlockSpec(values.shape, lambda i, w: (0, 0)),
            ],
            out_specs=pl.BlockSpec(memory_space=pl.ANY),
            scratch_shapes=[pltpu.SemaphoreType.DMA],
        ),
        name="pick_blocks",
    )(wanted, keys, values)


def attend_kernel(slots, q_ref, k_ref, v_ref, *rest):
    far = rest[: PICKED_BLOCKS - 1]
    out_ref, q_buf, k_buf, v_buf = rest[PICKED_BLOCKS - 1 :]
    heads = q_ref.shape[1] // HEAD_SIZE
    for h in range(heads):
        q_buf[pl.ds(h * BLOCK_TOKENS, BLOCK_TOKENS), :] = q_ref[:, pl.ds(h * HEAD_SIZE, HEAD_SIZE)]
    k_buf[pl.ds(0, BLOCK_TOKENS), :] = k_ref[...]
    v_buf[pl.ds(0, BLOCK_TOKENS), :] = v_ref[...]
    for j, block in enumerate(far):
        rows = pl.ds((j + 1) * BLOCK_TOKENS, BLOCK_TOKENS)
        k_buf[rows, :] = block[0, pl.ds(0, BLOCK_TOKENS), :]
        v_buf[rows, :] = block[0, pl.ds(BLOCK_TOKENS, BLOCK_TOKENS), :]
    factor = math.log2(math.e) / math.sqrt(HEAD_SIZE)
    shape = (BLOCK_TOKENS, BLOCK_TOKENS)
    causal = lax.broadcasted_iota(jnp.int32, shape, 1) <= lax.broadcasted_iota(jnp.int32, shape, 0)
    for h in range(heads):
        scores = lax.dot_general(
            q_buf[pl.ds(h * BLOCK_TOKENS, BLOCK_TOKENS), :],
            k_buf[...],
            (((1,), (1,)), ((), ())),
            preferred_element_type=jnp.float32,
        )
        own = jnp.where(causal, scores[:, :BLOCK_TOKENS], -jnp.inf)
        scores = jnp.concatenate([own, scores[:, BLOCK_TOKENS:]], axis=1)
        row_max = jnp.max(scores, axis=1, keepdims=True)
        exponents = jnp.exp2((scores - row_max) * factor)
        totals = jnp.sum(exponents, axis=1, keepdims=True)
        blended = jnp.dot(
            exponents.astype(jnp.bfloat16), v_buf[...], preferred_element_type=jnp.float32
        )
        out_ref[:, pl.ds(h * HEAD_SIZE, HEAD_SIZE)] = (blended / totals).astype(out_ref.dtype)


def attend(slots, queries, keys, values, fetched):
    rows, width = queries.shape
    blocks = rows // BLOCK_TOKENS
    span = PICKED_BLOCKS * BLOCK_TOKENS

    def far_spec(j):
        return pl.BlockSpec(
            (1, 2 * BLOCK_TOKENS, HEAD_SIZE), lambda i, s: (s[i * PICKED_BLOCKS + j], 0, 0)
        )

    return pl.pallas_call(
        attend_kernel,
        out_shape=jax.ShapeDtypeStruct((rows, width), jnp.bfloat16),
        grid_spec=pltpu.PrefetchScalarGridSpec(
            num_scalar_prefetch=1,
            grid=(blocks,),
            in_specs=[
                pl.BlockSpec((BLOCK_TOKENS, width), lambda i, s: (i, 0)),
                pl.BlockSpec((BLOCK_TOKENS, HEAD_SIZE), lambda i, s: (i, 0)),
                pl.BlockSpec((BLOCK_TOKENS, HEAD_SIZE), lambda i, s: (i, 0)),
            ]
            + [far_spec(j) for j in range(1, PICKED_BLOCKS)],
            out_specs=pl.BlockSpec((BLOCK_TOKENS, width), lambda i, s: (i, 0)),
            scratch_shapes=[
                pltpu.VMEM((width // HEAD_SIZE * BLOCK_TOKENS, HEAD_SIZE), jnp.bfloat16),
                pltpu.VMEM((span, HEAD_SIZE), jnp.bfloat16),
                pltpu.VMEM((span, HEAD_SIZE), jnp.bfloat16),
            ],
        ),
        name="attend",
    )(slots, queries, keys, values, *([fetched] * (PICKED_BLOCKS - 1)))


def body(queries, key_vector_rows, value_vector_rows, block_picks):
    peers = lax.axis_size("ctx")
    tok_dev = key_vector_rows.shape[0]
    blocks = tok_dev // BLOCK_TOKENS
    owners = block_picks // blocks
    local_ids = block_picks % blocks
    far_owners = owners[:, 1:].reshape(-1)
    far_ids = local_ids[:, 1:].reshape(-1)
    hits = far_owners[None, :] == jnp.arange(peers, dtype=jnp.int32)[:, None]
    requests = jnp.max(jnp.where(hits, far_ids[None, :], 0), axis=1)
    wanted = lax.all_to_all(requests, "ctx", split_axis=0, concat_axis=0, tiled=True)
    outgoing = pick_blocks(wanted, key_vector_rows, value_vector_rows)
    incoming = lax.all_to_all(outgoing, "ctx", split_axis=0, concat_axis=0, tiled=True)
    attended = attend(
        owners.reshape(-1), queries, key_vector_rows, value_vector_rows, incoming
    )
    return lax.all_to_all(attended, "kvh", split_axis=0, concat_axis=1, tiled=True)


def solution(mesh):
    return jax.shard_map(
        body,
        mesh=mesh,
        in_specs=(P("ctx", "kvh"), P("ctx", "kvh"), P("ctx", "kvh"), P("ctx", None)),
        out_specs=P(("ctx", "kvh"), None),
        check_vma=False,
    )
```

time: 327 us -> 184 us (0.56)
  waiting for transfers between devices: 185 us -> 95.3 us
  blocking collectives: 93.5 us -> 59.3 us
  local copies, waits for them, and re-layouts: 24.2 us -> 2.04 us
  Pallas kernels: 0 us -> 18.3 us
  matrix products: 10.1 us -> 0 us
  other arithmetic: 6.97 us -> 2.52 us
    all_to_all x1, waiting for transfers between devices: 185 us -> 95.3 us  [body(): lax.all_to_all(outgoing, 'ctx', split_axis=0, concat_axis=0, tiled=True)]
    all_gather x1 -> x0, blocking collectives: 57.4 us -> none  [body(): pick_table = lax.all_gather(block_picks, 'ctx', axis=0, tiled=True)]
    all_to_all x0 -> x1, blocking collectives: none -> 23.9 us  [body(): lax.all_to_all(requests, 'ctx', split_axis=0, concat_axis=0, tiled=True)]
    pallas_call x0 -> x2, Pallas kernels: none -> 18.3 us  [the longest x1 14.7 us: attend(): pl.pallas_call(attend_kernel, out_shape=jax.ShapeDtypeStruct((rows, width...]
    gather x2 -> x0, local copies, waits for them, and re-layouts: 11.7 us -> none  [the longest x1 6.3 us: body(): outgoing = local_kv[wanted]]
    dot_general x9 -> x0, matrix products: 10.1 us -> none  [the longest x4 4.5 us: block_attention(): jnp.einsum('gxqk,kgd->qgxd', weights, value_selection, preferred_element_...]
    dynamic_slice x12 -> x0, local copies, waits for them, and re-layouts: 4.71 us -> none  [body(): lax.map(attend_pair, (queries.reshape(blocks, BLOCK_TOKENS, -1), chosen))]
    reduce_sum x5 -> x0, other arithmetic: 3.62 us -> none  [the longest x4 3.44 us: block_attention(): totals = jnp.sum(exponents, axis=-1, keepdims=True)]
where the time goes in v1:
time: 184 us; the launch traced here: 183 us
  waiting for transfers between devices  95.3 us (52%)
  blocking collectives  59.3 us (32%)
  Pallas kernels  18.3 us (10%)
  starting transfers between devices  5.7 us (3%)
  other arithmetic  2.52 us (1%)
  local copies, waits for them, and re-layouts  2.04 us (1%)
    all_to_all x1, waiting for transfers between devices, body(): lax.all_to_all(outgoing, 'ctx', split_axis=0, concat_axis=0, tiled=True)  95.3 us
    all_to_all x1, blocking collectives, body(): lax.all_to_all(attended, 'kvh', split_axis=0, concat_axis=1, tiled=True)  35.3 us
    all_to_all x1, blocking collectives, body(): lax.all_to_all(requests, 'ctx', split_axis=0, concat_axis=0, tiled=True)  23.9 us
    pallas_call x1, Pallas kernels, attend(): pl.pallas_call(attend_kernel, out_shape=jax.ShapeDtypeStruct((rows, width...  14.7 us
    all_to_all x1, starting transfers between devices, body(): lax.all_to_all(outgoing, 'ctx', split_axis=0, concat_axis=0, tiled=True)  5.7 us
  transfers between devices with their start and end apart: 1, of which 1 were waited for; matrix products, arithmetic and copies ran while one was open for 0% of the time, Pallas kernels for 0%

profile of v1, /device:TPU:1, one launch (start us, length us, event | category | flops | bytes accessed | tf_op | source)
XLA Modules:
  0.0 183.2 jit_solution(9144673519828225347)
XLA Ops:
  0.0 0.7 add_select_fusion
  0.7 0.1 slice.7
  0.8 0.1 broadcast_in_dim.15
  0.9 0.1 slice.6
  0.9 0.1 eq.17
  1.0 0.1 select_reduce_fusion
  1.1 0.1 copy.10
  1.2 23.9 %all_to_all.35 = s32[64,1,1]{2,1,0:T(1,128)S(1)} all-to-all(s32[64,1,1]{2,1,0:T(1,128)S(1)} %copy.10), channel_id=1, replica_groups=mesh['ctx'=64,'kvh'=8] {'ctx'}, dimensions={0} | all-to-all | bytes 512 | tf_op jit(solution)/shard_map/all_to_all | solution.py:133
  25.1 1.7 reduce.wanted
  26.9 3.6 %pick_blocks.1 = bf16[64,256,128]{2,1,0:T(8,128)(2,1)} custom-call(s32[64]{0:T(128)} %reduce.wanted, bf16[512,128]{1,0:T(8,128)(2,1)} %k_ref.3, bf16[512,128]{1,0:T(8,128)(2,1)} %v_ref.3), custom_call_target="tpu_custom_call" | custom-call | tf_op jit(solution)/shard_map/pick_blocks/pallas_call | solution.py:40
  30.5 5.7 %all-to-all-start.1 = ((bf16[64,256,128]{2,1,0:T(8,128)(2,1)}), bf16[64,256,128]{2,1,0:T(8,128)(2,1)}, u32[]{:S(2)}, u32[]{:S(2)}) async-start(bf16[64,256,128]{2,1,0:T(8,128)(2,1)} %pick_blocks.1), calls=%async_computation.1 | async-start | bytes 8388608 | tf_op jit(solution)/shard_map/all_to_all | solution.py:135
  36.2 0.6 reshape.10.slots
  36.8 95.3 %all-to-all-done.1.rest_0_.rest_1_.rest_2_.rest_3_.rest_4_.rest_5_.rest_6_ = bf16[64,256,128]{2,1,0:T(8,128)(2,1)} async-done(((bf16[64,256,128]{2,1,0:T(8,128)(2,1)}), bf16[64,256,128]{2,1,0:T(8,128)(2,1)}, u32[]{:S(2)}, u32[]{:S(2)}) %all-to-all-start.1) | async-done | bytes 4194336 | tf_op jit(solution)/shard_map/all_to_all | solution.py:135
  132.1 14.7 %attend.1 = bf16[512,1024]{1,0:T(8,128)(2,1)} custom-call(s32[32]{0:T(128)} %reshape.10.slots, bf16[512,1024]{1,0:T(8,128)(2,1)} %q_ref.1, bf16[512,128]{1,0:T(8,128)(2,1)} %k_ref.3, bf16[512,128]{1,0:T(8,128)(2,1)} %v_ref.3, bf16[64,256,128]{2,1,0:T(8,128)(2,1)} %all-to-all-done.1.rest_0_.rest_1_.rest_2_.rest_3_.rest_4_.rest_5_.rest_6_, ...), custom_call_target="tpu_custom_call" | custom-call | tf_op jit(solution)/shard_map/attend/pallas_call | solution.py:100
  146.8 35.3 %all_to_all.36 = bf16[8,64,1024]{2,1,0:T(8,128)(2,1)S(1)} all-to-all(bf16[8,64,1024]{2,1,0:T(8,128)(2,1)} %bitcast.5), channel_id=1, replica_groups=mesh['ctx'=64,'kvh'=8] {'kvh'}, dimensions={0} | all-to-all | bytes 2097152 | tf_op jit(solution)/shard_map/all_to_all | solution.py:139
  182.1 1.1 copy.12
Async XLA Ops:
  30.5 101.6 %all-to-all-start.1 = ((bf16[64,256,128]{2,1,0:T(8,128)(2,1)}), bf16[64,256,128]{2,1,0:T(8,128)(2,1)}, u32[]{:S(2)}, u32[]{:S(2)}) async-start(bf16[64,256,128]{2,1,0:T(8,128)(2,1)} %pick_blocks.1), calls=%async_computation.1 | async-start | bytes 8388608 | tf_op jit(solution)/shard_map/all_to_all | solution.py:135

commit v2 on v1

v2 whole, which is shorter than its diff:
```python
import math

import jax
import jax.numpy as jnp
from jax import lax
from jax.experimental import pallas as pl
from jax.experimental.pallas import tpu as pltpu
from jax.sharding import PartitionSpec as P

HEAD_SIZE = 128
BLOCK_TOKENS = 128
PICKED_BLOCKS = 8
SIZE_X, SIZE_Z, CORES = 4, 8, 2
STEPS = (0, 1, 7, 2, 6, 3, 5, 4)
BATCHES = ((0, 1, 2), (3, 4, 5, 6, 7))


def pick_kernel(slots, wanted, *refs):
    shards, out_ref, sem = refs[:-2], refs[-2], refs[-1]
    half = shards[0].shape[0] // 2

    @pl.loop(0, out_ref.shape[0])
    def _(d):
        for n, (slot, shard) in enumerate(zip(slots, shards)):
            start = wanted[d * SIZE_Z + slot] * BLOCK_TOKENS
            for part in range(2):
                rows = pl.ds(pl.multiple_of(part * half + start, BLOCK_TOKENS), BLOCK_TOKENS)
                target = out_ref.at[d, n, pl.ds(part * BLOCK_TOKENS, BLOCK_TOKENS)]
                pltpu.make_async_copy(shard.at[rows], target, sem).start()

    pltpu.make_async_copy(out_ref, out_ref, sem).wait()


def pick_blocks(wanted, slots, shards):
    group = SIZE_X * CORES
    shape = (group, len(slots), 2 * BLOCK_TOKENS, HEAD_SIZE)
    return pl.pallas_call(
        lambda *refs: pick_kernel(slots, *refs),
        out_shape=jax.ShapeDtypeStruct(shape, shards[0].dtype),
        grid_spec=pltpu.PrefetchScalarGridSpec(
            num_scalar_prefetch=1,
            grid=(1,),
            in_specs=[pl.BlockSpec(s.shape, lambda i, w: (0, 0)) for s in shards],
            out_specs=pl.BlockSpec(memory_space=pl.ANY),
            scratch_shapes=[pltpu.SemaphoreType.DMA],
        ),
        cost_estimate=pl.CostEstimate(flops=0, bytes_accessed=2 * 2 * math.prod(shape), transcendentals=0),
        name="pick_blocks",
    )(wanted, *shards)


def attend_kernel(sizes, places, q_ref, k_ref, v_ref, *rest):
    fetched = rest[: len(sizes)]
    out_ref, q_buf, k_buf, v_buf, k_sem, v_sem = rest[len(sizes) :]
    row = pl.program_id(0)
    heads = q_ref.shape[1] // HEAD_SIZE

    def start(source, r, j):
        rows = pl.ds(j * BLOCK_TOKENS, BLOCK_TOKENS)
        pltpu.make_async_copy(source(0), k_buf.at[r, rows], k_sem.at[r]).start()
        pltpu.make_async_copy(source(1), v_buf.at[r, rows], v_sem.at[r]).start()

    @pl.when(row == 0)
    def _():
        for r in range(k_buf.shape[0]):
            own = pl.ds(r * BLOCK_TOKENS, BLOCK_TOKENS)
            start(lambda part: (k_ref, v_ref)[part].at[own], r, 0)
            for j in range(1, PICKED_BLOCKS):
                place = places[r * PICKED_BLOCKS + j]
                column, slot = place // SIZE_Z, place % SIZE_Z
                first = 0
                for ref, size in zip(fetched, sizes):
                    def go(ref=ref, first=first, r=r, j=j, column=column, slot=slot):
                        start(lambda part: ref.at[column, slot - first, pl.ds(part * BLOCK_TOKENS, BLOCK_TOKENS)], r, j)

                    if len(sizes) == 1:
                        go()
                    else:
                        pl.when((slot >= first) & (slot < first + size))(go)
                    first += size

    for h in range(heads):
        q_buf[pl.ds(h * BLOCK_TOKENS, BLOCK_TOKENS), :] = q_ref[:, pl.ds(h * HEAD_SIZE, HEAD_SIZE)]
    pltpu.make_async_copy(k_buf.at[row], k_buf.at[row], k_sem.at[row]).wait()
    pltpu.make_async_copy(v_buf.at[row], v_buf.at[row], v_sem.at[row]).wait()
    factor = math.log2(math.e) / math.sqrt(HEAD_SIZE)
    PAIR = 2
    shape = (PAIR * BLOCK_TOKENS, BLOCK_TOKENS)
    causal = lax.broadcasted_iota(jnp.int32, shape, 1) <= lax.broadcasted_iota(jnp.int32, shape, 0) % BLOCK_TOKENS
    for h in range(0, heads, PAIR):
        scores = lax.dot_general(
            q_buf[pl.ds(h * BLOCK_TOKENS, PAIR * BLOCK_TOKENS), :],
            k_buf[row],
            (((1,), (1,)), ((), ())),
            preferred_element_type=jnp.float32,
        )
        own = jnp.where(causal, scores[:, :BLOCK_TOKENS], -jnp.inf)
        scores = jnp.concatenate([own, scores[:, BLOCK_TOKENS:]], axis=1)
        row_max = jnp.max(scores, axis=1, keepdims=True)
        exponents = jnp.exp2((scores - row_max) * factor)
        totals = jnp.sum(exponents, axis=1, keepdims=True)
        blended = jnp.dot(exponents.astype(jnp.bfloat16), v_buf[row], preferred_element_type=jnp.float32)
        result = (blended / totals).astype(out_ref.dtype)
        for n in range(PAIR):
            out_ref[:, pl.ds((h + n) * HEAD_SIZE, HEAD_SIZE)] = result[n * BLOCK_TOKENS : (n + 1) * BLOCK_TOKENS]


def attend(places, queries, keys, values, fetched):
    rows, width = queries.shape
    blocks = rows // BLOCK_TOKENS
    span = PICKED_BLOCKS * BLOCK_TOKENS
    sizes = [f.shape[1] for f in fetched]
    anywhere = pl.BlockSpec(memory_space=pl.ANY)
    return pl.pallas_call(
        lambda *refs: attend_kernel(sizes, *refs),
        out_shape=jax.ShapeDtypeStruct((rows, width), jnp.bfloat16),
        grid_spec=pltpu.PrefetchScalarGridSpec(
            num_scalar_prefetch=1,
            grid=(blocks,),
            in_specs=[pl.BlockSpec((BLOCK_TOKENS, width), lambda i, s: (i, 0))] + [anywhere] * (2 + len(fetched)),
            out_specs=pl.BlockSpec((BLOCK_TOKENS, width), lambda i, s: (i, 0)),
            scratch_shapes=[
                pltpu.VMEM((width // HEAD_SIZE * BLOCK_TOKENS, HEAD_SIZE), jnp.bfloat16),
                pltpu.VMEM((blocks, span, HEAD_SIZE), jnp.bfloat16),
                pltpu.VMEM((blocks, span, HEAD_SIZE), jnp.bfloat16),
                pltpu.SemaphoreType.DMA((blocks,)),
                pltpu.SemaphoreType.DMA((blocks,)),
            ],
        ),
        name="attend",
    )(places, queries, keys, values, *fetched)


def flat(x, z, c):
    return (x % SIZE_X * SIZE_Z + z % SIZE_Z) * CORES + c


CHIPS = [(x, z, c) for x in range(SIZE_X) for z in range(SIZE_Z) for c in range(CORES)]
UP = [(flat(x, z, c), flat(x, z + 1, c)) for x, z, c in CHIPS]
DOWN = [(flat(x, z, c), flat(x, z - 1, c)) for x, z, c in CHIPS]
LAST = [(flat(x, z, c), flat(x, z + 1 - 2 * c, c)) for x, z, c in CHIPS]
ROWS = [[flat(x, z, c) for x in range(SIZE_X) for c in range(CORES)] for z in range(SIZE_Z)]


def to_row(array):
    return lax.all_to_all(array, "ctx", split_axis=0, concat_axis=0, axis_index_groups=ROWS, tiled=True)


def body(queries, key_vector_rows, value_vector_rows, block_picks):
    blocks = key_vector_rows.shape[0] // BLOCK_TOKENS
    group = SIZE_X * CORES
    me = lax.axis_index("ctx")
    my_z, my_core = me // CORES % SIZE_Z, me % CORES
    owners, local_ids = block_picks // blocks, block_picks % blocks
    column = owners // (SIZE_Z * CORES) * CORES + owners % CORES
    behind = (my_z - owners // CORES) % SIZE_Z
    slot = jnp.zeros_like(behind)
    for s, step in enumerate(STEPS):
        slot = jnp.where(behind == step, s, slot)
    places = column * SIZE_Z + slot
    far, far_ids = places[:, 1:].reshape(1, -1), local_ids[:, 1:].reshape(1, -1)
    hits = far == jnp.arange(group * SIZE_Z, dtype=jnp.int32)[:, None]
    requests = jnp.max(jnp.where(hits, far_ids, 0), axis=1).reshape(group, SIZE_Z)
    wanted = to_row(requests).reshape(-1)

    shard = jnp.concatenate([key_vector_rows, value_vector_rows], axis=0)
    held = {0: shard}
    for d in range(1, 4):
        held[d] = lax.ppermute(held[d - 1], "ctx", UP)
        held[8 - d] = lax.ppermute(held[(9 - d) % 8], "ctx", DOWN)
    held[4] = lax.ppermute(jnp.where(my_core == 0, held[3], held[5]), "ctx", LAST)

    fetched = []
    for slots in BATCHES:
        outgoing = pick_blocks(wanted, slots, [held[STEPS[s]] for s in slots])
        fetched.append(to_row(outgoing))
    attended = attend(places.reshape(-1), queries, key_vector_rows, value_vector_rows, fetched)
    return lax.all_to_all(attended, "kvh", split_axis=0, concat_axis=1, tiled=True)


def solution(mesh):
    return jax.shard_map(
        body,
        mesh=mesh,
        in_specs=(P("ctx", "kvh"), P("ctx", "kvh"), P("ctx", "kvh"), P("ctx", None)),
        out_specs=P(("ctx", "kvh"), None),
        check_vma=False,
    )
```

time: 184 us -> 161 us (0.88)
  waiting for transfers between devices: 95.3 us -> 43.2 us
  starting transfers between devices: 5.7 us -> 43.6 us
  blocking collectives: 59.3 us -> 43.5 us
  local copies, waits for them, and re-layouts: 2.04 us -> 9.9 us
    all_to_all x1 -> x2, waiting for transfers between devices: 95.3 us -> 31.2 us  [to_row(): lax.all_to_all(array, 'ctx', split_axis=0, concat_axis=0, axis_index_grou...]
    ppermute x0 -> x7, starting transfers between devices: none -> 31.7 us  [the longest x3 17.7 us: body(): held[8 - d] = lax.ppermute(held[(9 - d) % 8], 'ctx', DOWN)]
    all_to_all x1, blocking collectives: 23.9 us -> 9.65 us  [to_row(): lax.all_to_all(array, 'ctx', split_axis=0, concat_axis=0, axis_index_grou...]
    ppermute x0 -> x7, waiting for transfers between devices: none -> 12 us  [the longest x3 7.77 us: body(): held[d] = lax.ppermute(held[d - 1], 'ctx', UP)]
    all_to_all x1 -> x2, starting transfers between devices: 5.7 us -> 11.9 us  [to_row(): lax.all_to_all(array, 'ctx', split_axis=0, concat_axis=0, axis_index_grou...]
    unnamed x0 -> x25, local copies, waits for them, and re-layouts: none -> 5.68 us
    pallas_call x2 -> x3, Pallas kernels: 18.3 us -> 18.2 us  [the longest x1 11.8 us: attend(): pl.pallas_call(lambda *refs: attend_kernel(sizes, *refs), out_shape=jax.S...]
  transfers between devices with their start and end apart: 1 -> 9, of which waited for: 1 -> 5; matrix products, arithmetic and copies ran while one was open for 0% -> 2% of each run, Pallas kernels for 0% -> 2%
where the time goes in v2:
time: 161 us; the launch traced here: 160 us
  starting transfers between devices  43.6 us (27%)
  blocking collectives  43.5 us (27%)
  waiting for transfers between devices  43.2 us (27%)
  Pallas kernels  18.2 us (11%)
  local copies, waits for them, and re-layouts  9.9 us (6%)
    all_to_all x1, blocking collectives, body(): lax.all_to_all(attended, 'kvh', split_axis=0, concat_axis=1, tiled=True)  33.9 us
    all_to_all x2, waiting for transfers between devices, to_row(): lax.all_to_all(array, 'ctx', split_axis=0, concat_axis=0, axis_index_grou...  31.2 us
    ppermute x3, starting transfers between devices, body(): held[8 - d] = lax.ppermute(held[(9 - d) % 8], 'ctx', DOWN)  17.7 us
    all_to_all x2, starting transfers between devices, to_row(): lax.all_to_all(array, 'ctx', split_axis=0, concat_axis=0, axis_index_grou...  11.9 us
    pallas_call x1, Pallas kernels, attend(): pl.pallas_call(lambda *refs: attend_kernel(sizes, *refs), out_shape=jax.S...  11.8 us
    all_to_all x1, blocking collectives, to_row(): lax.all_to_all(array, 'ctx', split_axis=0, concat_axis=0, axis_index_grou...  9.65 us
    ppermute x3, starting transfers between devices, body(): held[d] = lax.ppermute(held[d - 1], 'ctx', UP)  8.64 us
    ppermute x3, waiting for transfers between devices, body(): held[d] = lax.ppermute(held[d - 1], 'ctx', UP)  7.77 us
  transfers between devices with their start and end apart: 9, of which 5 were waited for; matrix products, arithmetic and copies ran while one was open for 2% of the time, Pallas kernels for 2%

profile of v2, /device:TPU:1, one launch (start us, length us, event | category | flops | bytes accessed | tf_op | source)
XLA Modules:
  0.0 160.2 jit_solution(10285862948177036666)
XLA Ops:
  0.0 0.9 constant_dynamic-update-slice_fusion.1
  0.9 0.9 constant_dynamic-update-slice_fusion.refs_1_
  1.9 4.8 %collective-permute-start = (bf16[1024,128]{1,0:T(8,128)(2,1)S(1)}, bf16[1024,128]{1,0:T(8,128)(2,1)S(1)}, u32[]{:S(2)}, u32[]{:S(2)}) collective-permute-start(bf16[1024,128]{1,0:T(8,128)(2,1)S(1)} %constant_dynamic-update-slice_fusion.refs_1_), channel_id=1, source_target_pairs={{0,16},{8,24},{16,32},{24,40},{32,48},{40,56},{48,64},{56,72},{64,... | collective-permute-start | bytes 786440 | tf_op jit(solution)/shard_map/ppermute | solution.py:169
  6.7 8.6 %collective-permute-start.1 = (bf16[1024,128]{1,0:T(8,128)(2,1)S(1)}, bf16[1024,128]{1,0:T(8,128)(2,1)S(1)}, u32[]{:S(2)}, u32[]{:S(2)}) collective-permute-start(bf16[1024,128]{1,0:T(8,128)(2,1)S(1)} %constant_dynamic-update-slice_fusion.refs_1_), channel_id=1, source_target_pairs={{0,112},{8,120},{16,0},{24,8},{32,16},{40,24},{48,32},{56,40},{64,... | collective-permute-start | bytes 786440 | tf_op jit(solution)/shard_map/ppermute | solution.py:170
  15.3 0.7 add_select_fusion
  16.5 9.6 %all_to_all.38 = s32[8,1,8]{2,1,0:T(1,128)S(1)} all-to-all(s32[8,1,8]{2,1,0:T(1,128)S(1)} %bitcast.7), channel_id=1, replica_groups={{0,8,128,136,256,264,384,392},{16,24,144,152,272,280,400,408},{32,40,16..., dimensions={0} | all-to-all | bytes 512 | tf_op jit(solution)/shard_map/all_to_all | solution.py:146
  26.2 0.6 broadcast.52
  26.8 0.7 reduce.3
  27.5 0.6 reshape.19.refs_0_
  28.1 0.7 copy-done.7
  28.8 0.7 copy-done.5
  29.5 2.9 %pick_blocks.2 = bf16[8,3,256,128]{3,2,1,0:T(8,128)(2,1)} custom-call(s32[64]{0:T(128)} %reshape.19.refs_0_, bf16[1024,128]{1,0:T(8,128)(2,1)} %copy-done.4, bf16[1024,128]{1,0:T(8,128)(2,1)} %copy-done.7, bf16[1024,128]{1,0:T(8,128)(2,1)} %copy-done.5), custom_call_target="tpu_custom_call" | custom-call | bytes 3145728 | tf_op jit(solution)/shard_map/pick_blocks/pallas_call | solution.py:37
  32.5 4.3 %all-to-all-start.1 = ((bf16[8,3,256,128]{3,2,1,0:T(8,128)(2,1)}), bf16[8,3,256,128]{3,2,1,0:T(8,128)(2,1)S(1)}, u32[]{:S(2)}, u32[]{:S(2)}) async-start(bf16[8,3,256,128]{3,2,1,0:T(8,128)(2,1)} %pick_blocks.2), calls=%async_computation.1 | async-start | bytes 3145728 | tf_op jit(solution)/shard_map/all_to_all | solution.py:146
  36.8 1.9 %collective-permute-start.2 = (bf16[1024,128]{1,0:T(8,128)(2,1)S(1)}, bf16[1024,128]{1,0:T(8,128)(2,1)S(1)}, u32[]{:S(2)}, u32[]{:S(2)}) collective-permute-start(bf16[1024,128]{1,0:T(8,128)(2,1)S(1)} %copy-done.8), channel_id=1, source_target_pairs={{0,16},{8,24},{16,32},{24,40},{32,48},{40,56},{48,64},{56,72},{64,... | collective-permute-start | bytes 786440 | tf_op jit(solution)/shard_map/ppermute | solution.py:169
  38.7 4.6 %collective-permute-start.3 = (bf16[1024,128]{1,0:T(8,128)(2,1)S(1)}, bf16[1024,128]{1,0:T(8,128)(2,1)S(1)}, u32[]{:S(2)}, u32[]{:S(2)}) collective-permute-start(bf16[1024,128]{1,0:T(8,128)(2,1)S(1)} %copy-done.6), channel_id=1, source_target_pairs={{0,112},{8,120},{16,0},{24,8},{32,16},{40,24},{48,32},{56,40},{64,... | collective-permute-start | bytes 786440 | tf_op jit(solution)/shard_map/ppermute | solution.py:170
  43.3 4.3 %collective-permute-done.2.refs_1_ = bf16[1024,128]{1,0:T(8,128)(2,1)S(1)} collective-permute-done((bf16[1024,128]{1,0:T(8,128)(2,1)S(1)}, bf16[1024,128]{1,0:T(8,128)(2,1)S(1)}, u32[]{:S(2)}, u32[]{:S(2)}) %collective-permute-start.2) | collective-permute-done | bytes 262176 | tf_op jit(solution)/shard_map/ppermute | solution.py:169
  47.6 1.9 %collective-permute-start.4 = (bf16[1024,128]{1,0:T(8,128)(2,1)S(1)}, bf16[1024,128]{1,0:T(8,128)(2,1)S(1)}, u32[]{:S(2)}, u32[]{:S(2)}) collective-permute-start(bf16[1024,128]{1,0:T(8,128)(2,1)S(1)} %collective-permute-done.2.refs_1_), channel_id=1, source_target_pairs={{0,16},{8,24},{16,32},{24,40},{32,48},{40,56},{48,64},{56,72},{64,... | collective-permute-start | bytes 786440 | tf_op jit(solution)/shard_map/ppermute | solution.py:169
  49.6 4.6 %collective-permute-start.5 = (bf16[1024,128]{1,0:T(8,128)(2,1)S(1)}, bf16[1024,128]{1,0:T(8,128)(2,1)S(1)}, u32[]{:S(2)}, u32[]{:S(2)}) collective-permute-start(bf16[1024,128]{1,0:T(8,128)(2,1)S(1)} %collective-permute-done.3.refs_2_), channel_id=1, source_target_pairs={{0,112},{8,120},{16,0},{24,8},{32,16},{40,24},{48,32},{56,40},{64,... | collective-permute-start | bytes 786440 | tf_op jit(solution)/shard_map/ppermute | solution.py:170
  54.2 3.4 %collective-permute-done.4.refs_3_ = bf16[1024,128]{1,0:T(8,128)(2,1)S(1)} collective-permute-done((bf16[1024,128]{1,0:T(8,128)(2,1)S(1)}, bf16[1024,128]{1,0:T(8,128)(2,1)S(1)}, u32[]{:S(2)}, u32[]{:S(2)}) %collective-permute-start.4) | collective-permute-done | bytes 262176 | tf_op jit(solution)/shard_map/ppermute | solution.py:169
  57.6 0.9 collective-permute-done.5.refs_4_
  58.6 5.3 %collective-permute-start.6 = (bf16[1024,128]{1,0:T(8,128)(2,1)S(1)}, bf16[1024,128]{1,0:T(8,128)(2,1)S(1)}, u32[]{:S(2)}, u32[]{:S(2)}) collective-permute-start(bf16[1024,128]{1,0:T(8,128)(2,1)S(1)} %broadcast_select_fusion), channel_id=1, source_target_pairs={{0,16},{8,120},{16,32},{24,8},{32,48},{40,24},{48,64},{56,40},{64,... | collective-permute-start | bytes 786440 | tf_op jit(solution)/shard_map/ppermute | solution.py:171
  63.9 3.3 %collective-permute-done.6.refs_5_ = bf16[1024,128]{1,0:T(8,128)(2,1)S(1)} collective-permute-done((bf16[1024,128]{1,0:T(8,128)(2,1)S(1)}, bf16[1024,128]{1,0:T(8,128)(2,1)S(1)}, u32[]{:S(2)}, u32[]{:S(2)}) %collective-permute-start.6) | collective-permute-done | bytes 262176 | tf_op jit(solution)/shard_map/ppermute | solution.py:171
  67.2 0.7 copy-done.11
  67.9 3.4 %pick_blocks.3 = bf16[8,5,256,128]{3,2,1,0:T(8,128)(2,1)} custom-call(s32[64]{0:T(128)} %reshape.19.refs_0_, bf16[1024,128]{1,0:T(8,128)(2,1)} %copy-done.9, bf16[1024,128]{1,0:T(8,128)(2,1)} %copy-done.10, bf16[1024,128]{1,0:T(8,128)(2,1)} %copy-done.2, bf16[1024,128]{1,0:T(8,128)(2,1)} %copy-done.3, bf16[1024,128]{1,0:T(8,128)(2,1)} %copy-done.11), custom_call_target="tpu_custom_call" | custom-call | bytes 5242880 | tf_op jit(solution)/shard_map/pick_blocks/pallas_call | solution.py:37
  71.4 1.2 copy-done.1
  72.5 7.6 %all-to-all-start.2 = ((bf16[8,5,256,128]{3,2,1,0:T(8,128)(2,1)}), bf16[8,5,256,128]{3,2,1,0:T(8,128)(2,1)S(1)}, u32[]{:S(2)}, u32[]{:S(2)}) async-start(bf16[8,5,256,128]{3,2,1,0:T(8,128)(2,1)} %pick_blocks.3), calls=%async_computation.2 | async-start | bytes 5242880 | tf_op jit(solution)/shard_map/all_to_all | solution.py:146
  80.1 0.6 reshape.18.refs_0_
  80.8 31.2 %all-to-all-done.2.refs_5_ = bf16[8,5,256,128]{3,2,1,0:T(8,128)(2,1)S(1)} async-done(((bf16[8,5,256,128]{3,2,1,0:T(8,128)(2,1)}), bf16[8,5,256,128]{3,2,1,0:T(8,128)(2,1)S(1)}, u32[]{:S(2)}, u32[]{:S(2)}) %all-to-all-start.2) | async-done | bytes 2621472 | tf_op jit(solution)/shard_map/all_to_all | solution.py:146
  112.0 1.5 copy-done
  113.5 11.8 %attend.1 = bf16[512,1024]{1,0:T(8,128)(2,1)} custom-call(s32[32]{0:T(128)} %reshape.18.refs_0_, bf16[512,1024]{1,0:T(8,128)(2,1)} %refs_1_.1, bf16[512,128]{1,0:T(8,128)(2,1)} %refs_2_.1, bf16[512,128]{1,0:T(8,128)(2,1)} %refs_3_.1, bf16[8,3,256,128]{3,2,1,0:T(8,128)(2,1)} %copy-done.1, bf16[8,5,256,128]{3,2,1,0:T(8,128)(2,1)} %copy-done), custom_call_target="tpu_custom_call" | custom-call | tf_op jit(solution)/shard_map/attend/pallas_call | solution.py:114
  125.3 33.9 %all_to_all.39 = bf16[8,64,1024]{2,1,0:T(8,128)(2,1)S(1)} all-to-all(bf16[8,64,1024]{2,1,0:T(8,128)(2,1)} %bitcast.6), channel_id=1, replica_groups=mesh['ctx'=64,'kvh'=8] {'kvh'}, dimensions={0} | all-to-all | bytes 2097152 | tf_op jit(solution)/shard_map/all_to_all | solution.py:178
  159.2 1.1 copy.10
  (30 shorter events, 0.6 us)
Async XLA Ops:
  1.8 26.3 %copy-start.4 = (bf16[1024,128]{1,0:T(8,128)(2,1)}, bf16[1024,128]{1,0:T(8,128)(2,1)S(1)}, u32[]{:S(2)}) copy-start(bf16[1024,128]{1,0:T(8,128)(2,1)S(1)} %constant_dynamic-update-slice_fusion.refs_1_) | copy-start | bytes 786436
  1.9 26.3 %collective-permute-start = (bf16[1024,128]{1,0:T(8,128)(2,1)S(1)}, bf16[1024,128]{1,0:T(8,128)(2,1)S(1)}, u32[]{:S(2)}, u32[]{:S(2)}) collective-permute-start(bf16[1024,128]{1,0:T(8,128)(2,1)S(1)} %constant_dynamic-update-slice_fusion.refs_1_), channel_id=1, source_target_pairs={{0,16},{8,24},{16,32},{24,40},{32,48},{40,56},{48,64},{56,72},{64,... | collective-permute-start | bytes 786440 | tf_op jit(solution)/shard_map/ppermute | solution.py:169
  6.7 21.4 %collective-permute-start.1 = (bf16[1024,128]{1,0:T(8,128)(2,1)S(1)}, bf16[1024,128]{1,0:T(8,128)(2,1)S(1)}, u32[]{:S(2)}, u32[]{:S(2)}) collective-permute-start(bf16[1024,128]{1,0:T(8,128)(2,1)S(1)} %constant_dynamic-update-slice_fusion.refs_1_), channel_id=1, source_target_pairs={{0,112},{8,120},{16,0},{24,8},{32,16},{40,24},{48,32},{56,40},{64,... | collective-permute-start | bytes 786440 | tf_op jit(solution)/shard_map/ppermute | solution.py:170
  28.1 0.7 copy-start.7
  28.8 0.7 copy-start.5
  32.5 4.3 %copy-start.8 = (bf16[1024,128]{1,0:T(8,128)(2,1)S(1)}, bf16[1024,128]{1,0:T(8,128)(2,1)}, u32[]{:S(2)}) copy-start(bf16[1024,128]{1,0:T(8,128)(2,1)} %copy-done.7) | copy-start | bytes 786436
  32.5 6.3 %copy-start.6 = (bf16[1024,128]{1,0:T(8,128)(2,1)S(1)}, bf16[1024,128]{1,0:T(8,128)(2,1)}, u32[]{:S(2)}) copy-start(bf16[1024,128]{1,0:T(8,128)(2,1)} %copy-done.5) | copy-start | bytes 786436
  32.5 38.9 %all-to-all-start.1 = ((bf16[8,3,256,128]{3,2,1,0:T(8,128)(2,1)}), bf16[8,3,256,128]{3,2,1,0:T(8,128)(2,1)S(1)}, u32[]{:S(2)}, u32[]{:S(2)}) async-start(bf16[8,3,256,128]{3,2,1,0:T(8,128)(2,1)} %pick_blocks.2), calls=%async_computation.1 | async-start | bytes 3145728 | tf_op jit(solution)/shard_map/all_to_all | solution.py:146
  36.8 10.8 %collective-permute-start.2 = (bf16[1024,128]{1,0:T(8,128)(2,1)S(1)}, bf16[1024,128]{1,0:T(8,128)(2,1)S(1)}, u32[]{:S(2)}, u32[]{:S(2)}) collective-permute-start(bf16[1024,128]{1,0:T(8,128)(2,1)S(1)} %copy-done.8), channel_id=1, source_target_pairs={{0,16},{8,24},{16,32},{24,40},{32,48},{40,56},{48,64},{56,72},{64,... | collective-permute-start | bytes 786440 | tf_op jit(solution)/shard_map/ppermute | solution.py:169
  38.7 10.8 %collective-permute-start.3 = (bf16[1024,128]{1,0:T(8,128)(2,1)S(1)}, bf16[1024,128]{1,0:T(8,128)(2,1)S(1)}, u32[]{:S(2)}, u32[]{:S(2)}) collective-permute-start(bf16[1024,128]{1,0:T(8,128)(2,1)S(1)} %copy-done.6), channel_id=1, source_target_pairs={{0,112},{8,120},{16,0},{24,8},{32,16},{40,24},{48,32},{56,40},{64,... | collective-permute-start | bytes 786440 | tf_op jit(solution)/shard_map/ppermute | solution.py:170
  47.6 19.6 %copy-start.9 = (bf16[1024,128]{1,0:T(8,128)(2,1)}, bf16[1024,128]{1,0:T(8,128)(2,1)S(1)}, u32[]{:S(2)}) copy-start(bf16[1024,128]{1,0:T(8,128)(2,1)S(1)} %collective-permute-done.2.refs_1_) | copy-start | bytes 786436
  47.6 10.0 %collective-permute-start.4 = (bf16[1024,128]{1,0:T(8,128)(2,1)S(1)}, bf16[1024,128]{1,0:T(8,128)(2,1)S(1)}, u32[]{:S(2)}, u32[]{:S(2)}) collective-permute-start(bf16[1024,128]{1,0:T(8,128)(2,1)S(1)} %collective-permute-done.2.refs_1_), channel_id=1, source_target_pairs={{0,16},{8,24},{16,32},{24,40},{32,48},{40,56},{48,64},{56,72},{64,... | collective-permute-start | bytes 786440 | tf_op jit(solution)/shard_map/ppermute | solution.py:169
  49.6 17.6 %copy-start.10 = (bf16[1024,128]{1,0:T(8,128)(2,1)}, bf16[1024,128]{1,0:T(8,128)(2,1)S(1)}, u32[]{:S(2)}) copy-start(bf16[1024,128]{1,0:T(8,128)(2,1)S(1)} %collective-permute-done.3.refs_2_) | copy-start | bytes 786436
  49.6 9.0 %collective-permute-start.5 = (bf16[1024,128]{1,0:T(8,128)(2,1)S(1)}, bf16[1024,128]{1,0:T(8,128)(2,1)S(1)}, u32[]{:S(2)}, u32[]{:S(2)}) collective-permute-start(bf16[1024,128]{1,0:T(8,128)(2,1)S(1)} %collective-permute-done.3.refs_2_), channel_id=1, source_target_pairs={{0,112},{8,120},{16,0},{24,8},{32,16},{40,24},{48,32},{56,40},{64,... | collective-permute-start | bytes 786440 | tf_op jit(solution)/shard_map/ppermute | solution.py:170
  57.6 9.6 %copy-start.2 = (bf16[1024,128]{1,0:T(8,128)(2,1)}, bf16[1024,128]{1,0:T(8,128)(2,1)S(1)}, u32[]{:S(2)}) copy-start(bf16[1024,128]{1,0:T(8,128)(2,1)S(1)} %collective-permute-done.4.refs_3_) | copy-start | bytes 786436
  58.5 8.7 %copy-start.3 = (bf16[1024,128]{1,0:T(8,128)(2,1)}, bf16[1024,128]{1,0:T(8,128)(2,1)S(1)}, u32[]{:S(2)}) copy-start(bf16[1024,128]{1,0:T(8,128)(2,1)S(1)} %collective-permute-done.5.refs_4_) | copy-start | bytes 786436
  58.6 8.6 %collective-permute-start.6 = (bf16[1024,128]{1,0:T(8,128)(2,1)S(1)}, bf16[1024,128]{1,0:T(8,128)(2,1)S(1)}, u32[]{:S(2)}, u32[]{:S(2)}) collective-permute-start(bf16[1024,128]{1,0:T(8,128)(2,1)S(1)} %broadcast_select_fusion), channel_id=1, source_target_pairs={{0,16},{8,120},{16,32},{24,8},{32,48},{40,24},{48,64},{56,40},{64,... | collective-permute-start | bytes 786440 | tf_op jit(solution)/shard_map/ppermute | solution.py:171
  67.2 0.7 copy-start.11
  71.4 1.2 copy-start.1
  72.5 39.4 %all-to-all-start.2 = ((bf16[8,5,256,128]{3,2,1,0:T(8,128)(2,1)}), bf16[8,5,256,128]{3,2,1,0:T(8,128)(2,1)S(1)}, u32[]{:S(2)}, u32[]{:S(2)}) async-start(bf16[8,5,256,128]{3,2,1,0:T(8,128)(2,1)} %pick_blocks.3), calls=%async_computation.2 | async-start | bytes 5242880 | tf_op jit(solution)/shard_map/all_to_all | solution.py:146
  112.0 1.5 copy-start

commit v3 on v2

v3 whole, which is shorter than its diff:
```python
import math

import jax
import jax.numpy as jnp
from jax import lax
from jax.experimental import pallas as pl
from jax.experimental.pallas import tpu as pltpu
from jax.sharding import PartitionSpec as P


HEAD_SIZE = 128
BLOCK_TOKENS = 128
PICKED_BLOCKS = 8
SIZE_X, SIZE_Z, CORES = 4, 8, 2
BATCHES = ((0, 1, 2), (3, 4, 5, 6, 7))


def pack_kernel(k_ref, v_ref, out_ref, sem):
    for b in range(out_ref.shape[0]):
        rows = pl.ds(b * BLOCK_TOKENS, BLOCK_TOKENS)
        for part, ref in enumerate((k_ref, v_ref)):
            target = out_ref.at[b, pl.ds(part * BLOCK_TOKENS, BLOCK_TOKENS)]
            pltpu.make_async_copy(ref.at[rows], target, sem).start()
    pltpu.make_async_copy(out_ref, out_ref, sem).wait()


def pack(keys, values):
    rows, width = keys.shape
    return pl.pallas_call(
        pack_kernel,
        out_shape=jax.ShapeDtypeStruct((rows // BLOCK_TOKENS, 2 * BLOCK_TOKENS, width), keys.dtype),
        in_specs=[pl.BlockSpec(memory_space=pl.ANY)] * 2,
        out_specs=pl.BlockSpec(memory_space=pltpu.VMEM),
        scratch_shapes=[pltpu.SemaphoreType.DMA],
        compiler_params=pltpu.CompilerParams(vmem_limit_bytes=PACK_GRANT),
        cost_estimate=pl.CostEstimate(flops=0, bytes_accessed=8 * rows * width, transcendentals=0),
        name="pack",
    )(keys, values)


def pick_kernel(slots, sources, wanted, *refs):
    shards, out_ref = refs[:-1], refs[-1]

    @pl.loop(0, out_ref.shape[0])
    def _(d):
        for n, (slot, (which, first)) in enumerate(zip(slots, sources)):
            out_ref[d, n] = shards[which][first + wanted[d, slot]]


GRANT = 16 * 2**20
PACK_GRANT = 60 * 2**20
ATTEND_GRANT = 48 * 2**20


def pick_blocks(wanted, slots, sources, shards):
    group = SIZE_X * CORES
    shape = (group, len(slots), 2 * BLOCK_TOKENS, HEAD_SIZE)
    return pl.pallas_call(
        lambda *refs: pick_kernel(slots, sources, *refs),
        out_shape=jax.ShapeDtypeStruct(shape, shards[0].dtype),
        grid_spec=pltpu.PrefetchScalarGridSpec(
            num_scalar_prefetch=1,
            in_specs=[pl.BlockSpec(memory_space=pltpu.VMEM)] * len(shards),
            out_specs=pl.BlockSpec(memory_space=pltpu.VMEM),
        ),
        compiler_params=pltpu.CompilerParams(vmem_limit_bytes=GRANT),
        cost_estimate=pl.CostEstimate(flops=0, bytes_accessed=4 * math.prod(shape), transcendentals=0),
        name="pick_blocks",
    )(wanted, *shards)


def attend_kernel(sizes, places, q_ref, k_ref, v_ref, *rest):
    fetched = rest[: len(sizes)]
    out_ref, q_buf, kv_buf, sem = rest[len(sizes) :]
    row = pl.program_id(0)
    heads = q_ref.shape[1] // HEAD_SIZE

    def fetch(r):
        side = lax.rem(r, 2)
        own = pl.ds(pl.multiple_of(r * BLOCK_TOKENS, BLOCK_TOKENS), BLOCK_TOKENS)
        for part, ref in enumerate((k_ref, v_ref)):
            target = kv_buf.at[side, 0, pl.ds(part * BLOCK_TOKENS, BLOCK_TOKENS)]
            pltpu.make_async_copy(ref.at[own], target, sem.at[side]).start()
        for j in range(1, PICKED_BLOCKS):
            place = places[r * PICKED_BLOCKS + j]
            column, slot = place // SIZE_Z, place % SIZE_Z
            first = 0
            for ref, size in zip(fetched, sizes):

                @pl.when((slot >= first) & (slot < first + size))
                def _(ref=ref, first=first):
                    source = ref.at[column, slot - first]
                    pltpu.make_async_copy(source, kv_buf.at[side, j], sem.at[side]).start()

                first += size

    @pl.when(row == 0)
    def _():
        fetch(0)

    for h in range(heads):
        q_buf[pl.ds(h * BLOCK_TOKENS, BLOCK_TOKENS), :] = q_ref[:, pl.ds(h * HEAD_SIZE, HEAD_SIZE)]
    side = lax.rem(row, 2)
    pltpu.make_async_copy(kv_buf.at[side], kv_buf.at[side], sem.at[side]).wait()

    @pl.when(row + 1 < pl.num_programs(0))
    def _():
        fetch(row + 1)

    span = PICKED_BLOCKS * BLOCK_TOKENS
    keys = kv_buf[side, :, pl.ds(0, BLOCK_TOKENS), :].reshape(span, HEAD_SIZE)
    values = kv_buf[side, :, pl.ds(BLOCK_TOKENS, BLOCK_TOKENS), :].reshape(span, HEAD_SIZE)
    factor = math.log2(math.e) / math.sqrt(HEAD_SIZE)
    PAIR = 2
    shape = (PAIR * BLOCK_TOKENS, BLOCK_TOKENS)
    causal = lax.broadcasted_iota(jnp.int32, shape, 1) <= lax.broadcasted_iota(jnp.int32, shape, 0) % BLOCK_TOKENS
    for h in range(0, heads, PAIR):
        scores = lax.dot_general(
            q_buf[pl.ds(h * BLOCK_TOKENS, PAIR * BLOCK_TOKENS), :],
            keys,
            (((1,), (1,)), ((), ())),
            preferred_element_type=jnp.float32,
        )
        own = jnp.where(causal, scores[:, :BLOCK_TOKENS], -jnp.inf)
        scores = jnp.concatenate([own, scores[:, BLOCK_TOKENS:]], axis=1)
        row_max = jnp.max(scores, axis=1, keepdims=True)
        exponents = jnp.exp2((scores - row_max) * factor)
        totals = jnp.sum(exponents, axis=1, keepdims=True)
        blended = jnp.dot(exponents.astype(jnp.bfloat16), values, preferred_element_type=jnp.float32)
        result = (blended / totals).astype(out_ref.dtype)
        for n in range(PAIR):
            out_ref[:, pl.ds((h + n) * HEAD_SIZE, HEAD_SIZE)] = result[n * BLOCK_TOKENS : (n + 1) * BLOCK_TOKENS]


def attend(places, queries, keys, values, fetched):
    rows, width = queries.shape
    blocks = rows // BLOCK_TOKENS
    sizes = [f.shape[1] for f in fetched]
    anywhere = pl.BlockSpec(memory_space=pl.ANY)
    return pl.pallas_call(
        lambda *refs: attend_kernel(sizes, *refs),
        out_shape=jax.ShapeDtypeStruct((rows, width), jnp.bfloat16),
        grid_spec=pltpu.PrefetchScalarGridSpec(
            num_scalar_prefetch=1,
            grid=(blocks,),
            in_specs=[pl.BlockSpec((BLOCK_TOKENS, width), lambda i, s: (i, 0))] + [anywhere] * (2 + len(fetched)),
            out_specs=pl.BlockSpec((BLOCK_TOKENS, width), lambda i, s: (i, 0)),
            scratch_shapes=[
                pltpu.VMEM((width // HEAD_SIZE * BLOCK_TOKENS, HEAD_SIZE), jnp.bfloat16),
                pltpu.VMEM((2, PICKED_BLOCKS, 2 * BLOCK_TOKENS, HEAD_SIZE), jnp.bfloat16),
                pltpu.SemaphoreType.DMA((2,)),
            ],
        ),
        compiler_params=pltpu.CompilerParams(vmem_limit_bytes=ATTEND_GRANT),
        name="attend",
    )(places, queries, keys, values, *fetched)


def flat(x, z, c):
    return (x % SIZE_X * SIZE_Z + z % SIZE_Z) * CORES + c


CHIPS = [(x, z, c) for x in range(SIZE_X) for z in range(SIZE_Z) for c in range(CORES)]
SWAP = [(flat(x, z, c), flat(x, z, 1 - c)) for x, z, c in CHIPS]
STEP = [(flat(x, z, c), flat(x, z + 1 - 2 * c, c)) for x, z, c in CHIPS]
ACROSS = [(flat(x, z, c), flat(x, z + 4 - 8 * c, c)) for x, z, c in CHIPS]
ROWS = [[flat(x, z, c) for x in range(SIZE_X) for c in range(CORES)] for z in range(SIZE_Z)]


def to_row(array):
    return lax.all_to_all(array, "ctx", split_axis=0, concat_axis=0, axis_index_groups=ROWS)


def attention(queries, key_vector_rows, value_vector_rows, block_picks):
    blocks = key_vector_rows.shape[0] // BLOCK_TOKENS
    group = SIZE_X * CORES
    my_z = lax.axis_index("ctx") // CORES % SIZE_Z
    owners, local_ids = block_picks // blocks, block_picks % blocks
    owner_x, owner_z, owner_core = owners // (SIZE_Z * CORES), owners // CORES % SIZE_Z, owners % CORES
    behind = (my_z - owner_z) % SIZE_Z
    ahead = behind > SIZE_Z // 2
    steps = jnp.where(ahead, SIZE_Z - behind, behind)
    direct = (behind == 0) | (behind == SIZE_Z // 2)
    holder_core = jnp.where(direct, owner_core, ahead.astype(jnp.int32))
    slot = jnp.where(behind == 0, 0, 2 * steps - 1 + (owner_core ^ holder_core))
    places = (owner_x * CORES + holder_core) * SIZE_Z + slot
    far, far_ids = places[:, 1:].reshape(1, -1), local_ids[:, 1:].reshape(1, -1)
    hits = far == jnp.arange(group * SIZE_Z, dtype=jnp.int32)[:, None]
    requests = jnp.max(jnp.where(hits, far_ids, 0), axis=1).reshape(group, SIZE_Z)
    wanted = to_row(requests)

    shard = pack(key_vector_rows, value_vector_rows)
    other = lax.ppermute(shard, "ctx", SWAP)
    ring = [jnp.concatenate([shard, other], axis=0)]
    for _ in range(1, 4):
        ring.append(lax.ppermute(ring[-1], "ctx", STEP))
    last = lax.ppermute(shard, "ctx", ACROSS)

    origin = {0: (ring[0], 0), 7: (last, 0)}
    for j in range(1, 4):
        origin[2 * j - 1], origin[2 * j] = (ring[j], 0), (ring[j], blocks)
    fetched = []
    for slots in BATCHES:
        arrays, sources = [], []
        for s in slots:
            array, first = origin[s]
            which = next((i for i, a in enumerate(arrays) if a is array), None)
            if which is None:
                which = len(arrays)
                arrays.append(array)
            sources.append((which, first))
        outgoing = pick_blocks(wanted, slots, sources, arrays)
        fetched.append(to_row(outgoing))
    attended = attend(places.reshape(-1), queries, key_vector_rows, value_vector_rows, fetched)
    return lax.all_to_all(attended, "kvh", split_axis=0, concat_axis=1, tiled=True)


def solution(mesh):
    return jax.shard_map(
        attention,
        mesh=mesh,
        in_specs=(P("ctx", "kvh"), P("ctx", "kvh"), P("ctx", "kvh"), P("ctx", None)),
        out_specs=P(("ctx", "kvh"), None),
        check_vma=False,
    )
```

time: 161 us -> 157 us (0.975)
  waiting for transfers between devices: 43.2 us -> 56.1 us
  local copies, waits for them, and re-layouts: 9.9 us -> 1.55 us
  starting transfers between devices: 43.6 us -> 36 us
    ppermute x7 -> x5, waiting for transfers between devices: 12 us -> 24.3 us  [the longest x1 14.9 us: attention(): last = lax.ppermute(shard, 'ctx', ACROSS)]
    ppermute x7 -> x5, starting transfers between devices: 31.7 us -> 24.4 us  [the longest x3 10.9 us: attention(): ring.append(lax.ppermute(ring[-1], 'ctx', STEP))]
    unnamed x25 -> x8, local copies, waits for them, and re-layouts: 5.68 us -> 0.01 us
    pallas_call x2 -> x3, Pallas kernels: 6.38 us -> 5.82 us  [the longest x2 4.24 us: pick_blocks(): pl.pallas_call(lambda *refs: pick_kernel(slots, sources, *refs), out_shap...]
  transfers between devices with their start and end apart: 9 -> 7, of which waited for: 5 -> 4; matrix products, arithmetic and copies ran while one was open for 2% -> 1% of each run, Pallas kernels for 2% -> 1%
where the time goes in v3:
time: 157 us; the launch traced here: 156 us
  waiting for transfers between devices  56.1 us (36%)
  blocking collectives  42.6 us (27%)
  starting transfers between devices  36 us (23%)
  Pallas kernels  17.5 us (11%)
  other arithmetic  1.81 us (1%)
    all_to_all x1, blocking collectives, attention(): lax.all_to_all(attended, 'kvh', split_axis=0, concat_axis=1, tiled=True)  33.8 us
    all_to_all x2, waiting for transfers between devices, to_row(): lax.all_to_all(array, 'ctx', split_axis=0, concat_axis=0, axis_index_grou...  31.8 us
    ppermute x1, waiting for transfers between devices, attention(): last = lax.ppermute(shard, 'ctx', ACROSS)  14.9 us
    pallas_call x1, Pallas kernels, attend(): pl.pallas_call(lambda *refs: attend_kernel(sizes, *refs), out_shape=jax.S...  11.7 us
    all_to_all x2, starting transfers between devices, to_row(): lax.all_to_all(array, 'ctx', split_axis=0, concat_axis=0, axis_index_grou...  11.6 us
    ppermute x3, starting transfers between devices, attention(): ring.append(lax.ppermute(ring[-1], 'ctx', STEP))  10.9 us
    all_to_all x1, blocking collectives, to_row(): lax.all_to_all(array, 'ctx', split_axis=0, concat_axis=0, axis_index_grou...  8.81 us
    ppermute x1, starting transfers between devices, attention(): other = lax.ppermute(shard, 'ctx', SWAP)  8.75 us
  transfers between devices with their start and end apart: 7, of which 4 were waited for; matrix products, arithmetic and copies ran while one was open for 1% of the time, Pallas kernels for 1%

profile of v3, /device:TPU:1, one launch (start us, length us, event | category | flops | bytes accessed | tf_op | source)
XLA Modules:
  0.0 155.7 jit_solution(17141830692307323997)
XLA Ops:
  0.0 1.6 %pack.1 = bf16[4,256,128]{2,1,0:T(8,128)(2,1)} custom-call(bf16[512,128]{1,0:T(8,128)(2,1)} %refs_2_.1, bf16[512,128]{1,0:T(8,128)(2,1)} %refs_3_.1), custom_call_target="tpu_custom_call" | custom-call | bytes 524288 | tf_op jit(solution)/shard_map/pack/pallas_call | solution.py:29
  1.6 8.7 %collective-permute-start = (bf16[4,256,128]{2,1,0:T(8,128)(2,1)}, bf16[4,256,128]{2,1,0:T(8,128)(2,1)S(1)}, u32[]{:S(2)}, u32[]{:S(2)}) collective-permute-start(bf16[4,256,128]{2,1,0:T(8,128)(2,1)} %pack.1), channel_id=1, source_target_pairs={{0,8},{8,0},{16,24},{24,16},{32,40},{40,32},{48,56},{56,48},{64,72... | collective-permute-start | bytes 786440 | tf_op jit(solution)/shard_map/ppermute | solution.py:193
  10.3 1.4 collective-permute-done
  11.7 1.0 pad_maximum_fusion.refs_1_
  12.7 5.3 %collective-permute-start.1 = (bf16[8,256,128]{2,1,0:T(8,128)(2,1)S(1)}, bf16[8,256,128]{2,1,0:T(8,128)(2,1)S(1)}, u32[]{:S(2)}, u32[]{:S(2)}) collective-permute-start(bf16[8,256,128]{2,1,0:T(8,128)(2,1)S(1)} %pad_maximum_fusion.refs_1_), channel_id=1, source_target_pairs={{0,16},{8,120},{16,32},{24,8},{32,48},{40,24},{48,64},{56,40},{64,... | collective-permute-start | bytes 1572872 | tf_op jit(solution)/shard_map/ppermute | solution.py:196
  18.0 0.7 add_select_fusion
  18.8 0.1 slice.7
  18.8 0.1 broadcast_in_dim.17
  18.9 0.1 slice.6
  19.0 0.1 eq.31
  19.1 0.1 select_reduce_fusion
  19.2 0.1 all_to_all.27
  19.3 8.8 %all_to_all.40 = s32[8,1,8]{2,1,0:T(1,128)S(1)} all-to-all(s32[8,1,8]{2,1,0:T(1,128)S(1)} %bitcast.10), channel_id=1, replica_groups={{0,8,128,136,256,264,384,392},{16,24,144,152,272,280,400,408},{32,40,16..., dimensions={0} | all-to-all | bytes 512 | tf_op jit(solution)/shard_map/all_to_all | solution.py:171
  28.1 0.0 collective-permute-done.1.refs_2_
  28.1 1.9 %pick_blocks.2 = bf16[8,3,256,128]{3,2,1,0:T(8,128)(2,1)} custom-call(s32[8,8]{1,0:T(8,128)S(1)} %bitcast.7, bf16[8,256,128]{2,1,0:T(8,128)(2,1)S(1)} %pad_maximum_fusion.refs_1_, bf16[8,256,128]{2,1,0:T(8,128)(2,1)S(1)} %collective-permute-done.1.refs_2_), custom_call_target="tpu_custom_call" | custom-call | bytes 3145728 | tf_op jit(solution)/shard_map/pick_blocks/pallas_call | solution.py:58
  30.0 4.2 %all-to-all-start.1 = ((bf16[8,3,256,128]{3,2,1,0:T(8,128)(2,1)}), bf16[8,3,256,128]{3,2,1,0:T(8,128)(2,1)S(1)}, u32[]{:S(2)}, u32[]{:S(2)}) async-start(bf16[8,3,256,128]{3,2,1,0:T(8,128)(2,1)} %pick_blocks.2), calls=%async_computation.1 | async-start | bytes 3145728 | tf_op jit(solution)/shard_map/all_to_all | solution.py:171
  34.2 2.2 %collective-permute-start.2 = (bf16[8,256,128]{2,1,0:T(8,128)(2,1)S(1)}, bf16[8,256,128]{2,1,0:T(8,128)(2,1)S(1)}, u32[]{:S(2)}, u32[]{:S(2)}) collective-permute-start(bf16[8,256,128]{2,1,0:T(8,128)(2,1)S(1)} %collective-permute-done.1.refs_2_), channel_id=1, source_target_pairs={{0,16},{8,120},{16,32},{24,8},{32,48},{40,24},{48,64},{56,40},{64,... | collective-permute-start | bytes 1572872 | tf_op jit(solution)/shard_map/ppermute | solution.py:196
  36.3 8.0 %collective-permute-done.2.refs_1_ = bf16[8,256,128]{2,1,0:T(8,128)(2,1)S(1)} collective-permute-done((bf16[8,256,128]{2,1,0:T(8,128)(2,1)S(1)}, bf16[8,256,128]{2,1,0:T(8,128)(2,1)S(1)}, u32[]{:S(2)}, u32[]{:S(2)}) %collective-permute-start.2) | collective-permute-done | bytes 524320 | tf_op jit(solution)/shard_map/ppermute | solution.py:196
  44.4 3.4 %collective-permute-start.3 = (bf16[8,256,128]{2,1,0:T(8,128)(2,1)S(1)}, bf16[8,256,128]{2,1,0:T(8,128)(2,1)S(1)}, u32[]{:S(2)}, u32[]{:S(2)}) collective-permute-start(bf16[8,256,128]{2,1,0:T(8,128)(2,1)S(1)} %collective-permute-done.2.refs_1_), channel_id=1, source_target_pairs={{0,16},{8,120},{16,32},{24,8},{32,48},{40,24},{48,64},{56,40},{64,... | collective-permute-start | bytes 1572872 | tf_op jit(solution)/shard_map/ppermute | solution.py:196
  47.8 0.0 copy-done.3
  47.8 4.8 %collective-permute-start.4 = (bf16[4,256,128]{2,1,0:T(8,128)(2,1)S(1)}, bf16[4,256,128]{2,1,0:T(8,128)(2,1)S(1)}, u32[]{:S(2)}, u32[]{:S(2)}) collective-permute-start(bf16[4,256,128]{2,1,0:T(8,128)(2,1)S(1)} %copy-done.3), channel_id=1, source_target_pairs={{0,64},{8,72},{16,80},{24,88},{32,96},{40,104},{48,112},{56,120},{... | collective-permute-start | bytes 786440 | tf_op jit(solution)/shard_map/ppermute | solution.py:197
  52.6 14.9 %collective-permute-done.4.refs_3_ = bf16[4,256,128]{2,1,0:T(8,128)(2,1)S(1)} collective-permute-done((bf16[4,256,128]{2,1,0:T(8,128)(2,1)S(1)}, bf16[4,256,128]{2,1,0:T(8,128)(2,1)S(1)}, u32[]{:S(2)}, u32[]{:S(2)}) %collective-permute-start.4) | collective-permute-done | bytes 262176 | tf_op jit(solution)/shard_map/ppermute | solution.py:197
  67.5 0.0 collective-permute-done.3.refs_2_
  67.5 2.3 %pick_blocks.3 = bf16[8,5,256,128]{3,2,1,0:T(8,128)(2,1)} custom-call(s32[8,8]{1,0:T(8,128)S(1)} %bitcast.8, bf16[8,256,128]{2,1,0:T(8,128)(2,1)S(1)} %collective-permute-done.2.refs_1_, bf16[8,256,128]{2,1,0:T(8,128)(2,1)S(1)} %collective-permute-done.3.refs_2_, bf16[4,256,128]{2,1,0:T(8,128)(2,1)S(1)} %collective-permute-done.4.refs_3_), custom_call_target="tpu_custom_call" | custom-call | bytes 5242880 | tf_op jit(solution)/shard_map/pick_blocks/pallas_call | solution.py:58
  69.9 0.0 all-to-all-done.1.refs_4_
  69.9 7.4 %all-to-all-start.2 = ((bf16[8,5,256,128]{3,2,1,0:T(8,128)(2,1)}), bf16[8,5,256,128]{3,2,1,0:T(8,128)(2,1)}, u32[]{:S(2)}, u32[]{:S(2)}) async-start(bf16[8,5,256,128]{3,2,1,0:T(8,128)(2,1)} %pick_blocks.3), calls=%async_computation.2 | async-start | bytes 5242880 | tf_op jit(solution)/shard_map/all_to_all | solution.py:171
  77.3 0.1 reshape.14.refs_0_
  77.3 31.8 %all-to-all-done.2.refs_5_ = bf16[8,5,256,128]{3,2,1,0:T(8,128)(2,1)} async-done(((bf16[8,5,256,128]{3,2,1,0:T(8,128)(2,1)}), bf16[8,5,256,128]{3,2,1,0:T(8,128)(2,1)}, u32[]{:S(2)}, u32[]{:S(2)}) %all-to-all-start.2) | async-done | bytes 2621472 | tf_op jit(solution)/shard_map/all_to_all | solution.py:171
  109.2 0.0 copy-done.1
  109.2 11.7 %attend.1 = bf16[512,1024]{1,0:T(8,128)(2,1)S(1)} custom-call(s32[32]{0:T(128)S(1)} %reshape.14.refs_0_, bf16[512,1024]{1,0:T(8,128)(2,1)S(1)} %copy-done, bf16[512,128]{1,0:T(8,128)(2,1)S(1)} %copy-done.1, bf16[512,128]{1,0:T(8,128)(2,1)S(1)} %copy-done.2, bf16[8,3,256,128]{3,2,1,0:T(8,128)(2,1)S(1)} %all-to-all-done.1.refs_4_, ...), custom_call_target="tpu_custom_call" | custom-call | tf_op jit(solution)/shard_map/attend/pallas_call | solution.py:140
  120.9 33.8 %all_to_all.41 = bf16[8,64,1024]{2,1,0:T(8,128)(2,1)S(1)} all-to-all(bf16[8,64,1024]{2,1,0:T(8,128)(2,1)S(1)} %bitcast.6), channel_id=1, replica_groups=mesh['ctx'=64,'kvh'=8] {'kvh'}, dimensions={0} | all-to-all | bytes 2097152 | tf_op jit(solution)/shard_map/all_to_all | solution.py:215
  154.6 1.1 copy.10
  (6 shorter events, 0.0 us)
Async XLA Ops:
  1.6 10.1 %collective-permute-start = (bf16[4,256,128]{2,1,0:T(8,128)(2,1)}, bf16[4,256,128]{2,1,0:T(8,128)(2,1)S(1)}, u32[]{:S(2)}, u32[]{:S(2)}) collective-permute-start(bf16[4,256,128]{2,1,0:T(8,128)(2,1)} %pack.1), channel_id=1, source_target_pairs={{0,8},{8,0},{16,24},{24,16},{32,40},{40,32},{48,56},{56,48},{64,72... | collective-permute-start | bytes 786440 | tf_op jit(solution)/shard_map/ppermute | solution.py:193
  12.7 15.4 %collective-permute-start.1 = (bf16[8,256,128]{2,1,0:T(8,128)(2,1)S(1)}, bf16[8,256,128]{2,1,0:T(8,128)(2,1)S(1)}, u32[]{:S(2)}, u32[]{:S(2)}) collective-permute-start(bf16[8,256,128]{2,1,0:T(8,128)(2,1)S(1)} %pad_maximum_fusion.refs_1_), channel_id=1, source_target_pairs={{0,16},{8,120},{16,32},{24,8},{32,48},{40,24},{48,64},{56,40},{64,... | collective-permute-start | bytes 1572872 | tf_op jit(solution)/shard_map/ppermute | solution.py:196
  28.1 19.7 %copy-start.3 = (bf16[4,256,128]{2,1,0:T(8,128)(2,1)S(1)}, bf16[4,256,128]{2,1,0:T(8,128)(2,1)}, u32[]{:S(2)}) copy-start(bf16[4,256,128]{2,1,0:T(8,128)(2,1)} %pack.1) | copy-start | bytes 786436
  30.0 39.9 %all-to-all-start.1 = ((bf16[8,3,256,128]{3,2,1,0:T(8,128)(2,1)}), bf16[8,3,256,128]{3,2,1,0:T(8,128)(2,1)S(1)}, u32[]{:S(2)}, u32[]{:S(2)}) async-start(bf16[8,3,256,128]{3,2,1,0:T(8,128)(2,1)} %pick_blocks.2), calls=%async_computation.1 | async-start | bytes 3145728 | tf_op jit(solution)/shard_map/all_to_all | solution.py:171
  34.2 10.2 %collective-permute-start.2 = (bf16[8,256,128]{2,1,0:T(8,128)(2,1)S(1)}, bf16[8,256,128]{2,1,0:T(8,128)(2,1)S(1)}, u32[]{:S(2)}, u32[]{:S(2)}) collective-permute-start(bf16[8,256,128]{2,1,0:T(8,128)(2,1)S(1)} %collective-permute-done.1.refs_2_), channel_id=1, source_target_pairs={{0,16},{8,120},{16,32},{24,8},{32,48},{40,24},{48,64},{56,40},{64,... | collective-permute-start | bytes 1572872 | tf_op jit(solution)/shard_map/ppermute | solution.py:196
  44.4 23.1 %collective-permute-start.3 = (bf16[8,256,128]{2,1,0:T(8,128)(2,1)S(1)}, bf16[8,256,128]{2,1,0:T(8,128)(2,1)S(1)}, u32[]{:S(2)}, u32[]{:S(2)}) collective-permute-start(bf16[8,256,128]{2,1,0:T(8,128)(2,1)S(1)} %collective-permute-done.2.refs_1_), channel_id=1, source_target_pairs={{0,16},{8,120},{16,32},{24,8},{32,48},{40,24},{48,64},{56,40},{64,... | collective-permute-start | bytes 1572872 | tf_op jit(solution)/shard_map/ppermute | solution.py:196
  47.8 19.7 %collective-permute-start.4 = (bf16[4,256,128]{2,1,0:T(8,128)(2,1)S(1)}, bf16[4,256,128]{2,1,0:T(8,128)(2,1)S(1)}, u32[]{:S(2)}, u32[]{:S(2)}) collective-permute-start(bf16[4,256,128]{2,1,0:T(8,128)(2,1)S(1)} %copy-done.3), channel_id=1, source_target_pairs={{0,64},{8,72},{16,80},{24,88},{32,96},{40,104},{48,112},{56,120},{... | collective-permute-start | bytes 786440 | tf_op jit(solution)/shard_map/ppermute | solution.py:197
  69.9 39.3 %copy-start = (bf16[512,1024]{1,0:T(8,128)(2,1)S(1)}, bf16[512,1024]{1,0:T(8,128)(2,1)}, u32[]{:S(2)}) copy-start(bf16[512,1024]{1,0:T(8,128)(2,1)} %refs_1_.1) | copy-start | bytes 3145732
  69.9 39.3 %copy-start.1 = (bf16[512,128]{1,0:T(8,128)(2,1)S(1)}, bf16[512,128]{1,0:T(8,128)(2,1)}, u32[]{:S(2)}) copy-start(bf16[512,128]{1,0:T(8,128)(2,1)} %refs_2_.1) | copy-start | bytes 393220
  69.9 39.3 %copy-start.2 = (bf16[512,128]{1,0:T(8,128)(2,1)S(1)}, bf16[512,128]{1,0:T(8,128)(2,1)}, u32[]{:S(2)}) copy-start(bf16[512,128]{1,0:T(8,128)(2,1)} %refs_3_.1) | copy-start | bytes 393220
  69.9 39.3 %all-to-all-start.2 = ((bf16[8,5,256,128]{3,2,1,0:T(8,128)(2,1)}), bf16[8,5,256,128]{3,2,1,0:T(8,128)(2,1)}, u32[]{:S(2)}, u32[]{:S(2)}) async-start(bf16[8,5,256,128]{3,2,1,0:T(8,128)(2,1)} %pick_blocks.3), calls=%async_computation.2 | async-start | bytes 5242880 | tf_op jit(solution)/shard_map/all_to_all | solution.py:171
